TPU v7x, 256 devices: a whole 4x4x8 slice. The times are simulated.
256 devices in a mesh: dp: 32 (over x, y, core), tensor: 8 (over z).
Axes of the slice: x: 4, y: 4, z: 8, core: 2. Of those that a mesh axis runs over, the one named last changes fastest.
Arguments:
- output_gradient: bfloat16 [8192, 8192], P('dp', 'tensor'), may hold values from -96 to 96
- hidden: bfloat16 [8192, 28672], P('dp', 'tensor'), may hold values from -3 to 3
- adapter_down: bfloat16 [64, 16, 28672], P('dp', None, 'tensor'), may hold values from -0.03125 to 0.03125
- adapter_up: bfloat16 [64, 16, 8192], P('dp', None, 'tensor'), may hold values from -0.0625 to 0.0625
- counts: int32 [64], replicated, may hold values from 32 to 288, as said below
- offsets: int32 [64], replicated, may hold values from 0 to 8160, as said below
- adapter_slot: int32 [64], replicated, may hold values from 0 to 63, as said below
Outputs:
- adapter_hidden_gradient: bfloat16 [8192, 28672], P('dp', 'tensor')
- adapter_down_gradient: float32 [64, 16, 28672], P('dp', None, 'tensor')
- adapter_up_gradient: float32 [64, 16, 8192], P('dp', None, 'tensor')
Inputs may be any that keep to these rules, and one draw needn't show every extreme that they name: counts sum to 8192; the last adapter has exactly 32 tokens; exactly one adapter has 288 tokens, every other fewer. Tokens are grouped by adapter in increasing order: offsets[a] is the sum of counts of the adapters before a. `adapter_slot`: every slot holds exactly one adapter; slot k lies on dp index k // 2, and any 64 // 2 adapters in a row lie on distinct dp indices.
All inputs are finite; a program needn't handle non-finite values.
Results may differ from a plain program's by a relative error of at most 0.0075.
Values may be sent and summed in bfloat16 or wider, within the bound.
No kernel may reach another device: no remote copies, remote signals or barrier semaphores. Data moves between devices by JAX's collectives and lax.ppermute only.
A program may use at most 64 MiB of HBM per device.

v0:
```python
import jax
import jax.numpy as jnp
from jax import lax
from jax.sharding import PartitionSpec as P

adapter_factor = 2.0


def selected_rows(value_entries, shard_portion, member_rows):
    shard_count = shard_portion.shape[0]
    adapter_rank = shard_portion.shape[1]
    flattened_rows = shard_portion.reshape(shard_count * adapter_rank, shard_portion.shape[2])
    rank_scores = lax.dot_general(
        value_entries, flattened_rows, (((1,), (1,)), ((), ())), preferred_element_type=jnp.float32
    )
    selected_entries = member_rows.astype(jnp.float32)
    return jnp.sum(
        rank_scores.reshape(value_entries.shape[0], shard_count, adapter_rank)
        * selected_entries[:, :, None],
        axis=1,
    )


def on_device(output_gradient, hidden, adapter_down, adapter_up, counts, offsets, adapter_slot):
    total_rows = output_gradient.shape[0]
    slots_per_worker = adapter_down.shape[0]
    adapter_rank = adapter_down.shape[1]
    hidden_size_count = hidden.shape[1]
    dp_count = lax.axis_size("dp")
    adapter_list = slots_per_worker * dp_count
    first_token = lax.axis_index("dp") * total_rows
    positions = first_token + lax.broadcasted_iota(jnp.int32, (total_rows, 1), 0)
    inside = (positions >= offsets[None, :]) & (positions < (offsets + counts)[None, :])
    slot_of_row = jnp.sum(jnp.where(inside, adapter_slot[None, :], 0), axis=1)
    columns = lax.broadcasted_iota(jnp.int32, (1, adapter_list), 1)
    member_rows = (slot_of_row[:, None] == columns).astype(jnp.bfloat16)
    up_portion = selected_rows(
        output_gradient, lax.all_gather(adapter_up, "dp", axis=0, tiled=True), member_rows
    )
    up_incoming = lax.psum(up_portion, "tensor").astype(jnp.bfloat16)
    broadcast_up = member_rows[:, :, None] * up_incoming[:, None, :]
    shard_portion = lax.all_gather(adapter_down, "dp", axis=0, tiled=True)
    shard_count = shard_portion.shape[0]
    flattened_rows = shard_portion.reshape(shard_count * adapter_rank, hidden_size_count)
    down_partial = selected_rows(hidden, shard_portion, member_rows)
    broadcast_portion = broadcast_up
    broadcast_portion = broadcast_portion.reshape(total_rows, shard_count * adapter_rank)
    gradient_running = jnp.dot(
        broadcast_portion, flattened_rows, preferred_element_type=jnp.float32
    )
    down_partial, gradient_running = (down_partial, gradient_running)
    down_incoming = lax.psum(down_partial, "tensor").astype(jnp.bfloat16)
    adapter_hidden_gradient = (adapter_factor * gradient_running).astype(jnp.bfloat16)
    broadcast_down = member_rows[:, :, None] * down_incoming[:, None, :]

    def slot_term(spread, value_entries, shard_count):
        broadcast_portion = spread
        broadcast_portion = broadcast_portion.reshape(total_rows, shard_count * adapter_rank)
        matrix_product = lax.dot_general(
            broadcast_portion,
            value_entries,
            (((0,), (0,)), ((), ())),
            preferred_element_type=jnp.float32,
        )
        return matrix_product.reshape(shard_count, adapter_rank, value_entries.shape[1])

    down_reduced = lax.psum_scatter(
        slot_term(broadcast_up, hidden, slots_per_worker * lax.axis_size("dp")).astype(
            jnp.bfloat16
        ),
        "dp",
        scatter_dimension=0,
        tiled=True,
    ).astype(jnp.float32)
    up_reduced = lax.psum_scatter(
        slot_term(broadcast_down, output_gradient, slots_per_worker * lax.axis_size("dp")).astype(
            jnp.bfloat16
        ),
        "dp",
        scatter_dimension=0,
        tiled=True,
    ).astype(jnp.float32)
    slot_grid = adapter_slot[:, None] == columns
    total_slots = jnp.sum(jnp.where(slot_grid, counts[:, None], 0), axis=0)
    scale_entries = adapter_factor / total_slots.astype(jnp.float32)
    owner_scale = lax.dynamic_slice_in_dim(
        scale_entries, lax.axis_index("dp") * slots_per_worker, slots_per_worker, 0
    )
    adapter_down_gradient = down_reduced * owner_scale[:, None, None]
    adapter_up_gradient = up_reduced * owner_scale[:, None, None]
    return (adapter_hidden_gradient, adapter_down_gradient, adapter_up_gradient)


def solution(mesh):
    placed = (
        P("dp", "tensor"),
        P("dp", "tensor"),
        P("dp", None, "tensor"),
        P("dp", None, "tensor"),
        P(),
        P(),
        P(),
    )
    return jax.shard_map(
        on_device,
        mesh=mesh,
        in_specs=placed,
        out_specs=(P("dp", "tensor"), P("dp", None, "tensor"), P("dp", None, "tensor")),
        check_vma=False,
    )
```

profile of v0, /device:TPU:2, one launch (start us, length us, event | category | flops | bytes accessed | tf_op | source)
XLA Modules:
  0.0 353.9 jit_solution(15384436137109650157)
XLA Ops:
  7.2 0.0 all-gather.3.cloned.1.call-start
  7.2 0.7 all-gather.3.cloned.1.call-update
  7.9 0.0 all-gather.5.cloned.1.call-start
  8.0 0.7 all-gather.5.cloned.1.call-update
  8.7 0.0 reduce-scatter.5.cloned.1.call-start
  8.7 0.7 add.27
  9.4 0.8 select_reduce_fusion
  10.2 51.6 %all-gather.3.cloned.1.call-done = bf16[64,16,1024]{2,1,0:T(8,128)(2,1)} async-done(((bf16[2,16,1024]{2,1,0:T(8,128)(2,1)}), bf16[64,16,1024]{2,1,0:T(8,128)(2,1)}) %all-gather.3.cloned.1.call-update) | async-done | bytes 2097168 | tf_op jit(solution)/shard_map/all_gather | solution.py:38
  61.8 4.2 %fusion.16 = f32[256,16]{0,1:T(8,128)S(1)} fusion(bf16[64,16,1024]{2,1,0:T(8,128)(2,1)} %all-gather.3.cloned.1.call-done, bf16[256,1024]{1,0:T(8,128)(2,1)} %param.7, f32[256,64]{0,1:T(8,128)S(1)} %get-tuple-element.6), kind=kOutput, calls=%fused_computation.13 | convolution fusion | flops 537391104 | bytes 2703360 | tf_op jit(solution)/shard_map/dot_general | solution.py:13
  66.0 53.4 %all-gather.5.cloned.1.call-done = bf16[64,16,3584]{2,1,0:T(8,128)(2,1)} async-done(((bf16[2,16,3584]{2,1,0:T(8,128)(2,1)}), bf16[64,16,3584]{2,1,0:T(8,128)(2,1)}) %all-gather.5.cloned.1.call-update) | async-done | bytes 7340048 | tf_op jit(solution)/shard_map/all_gather | solution.py:42
  119.4 11.0 %fusion.19 = f32[256,16]{0,1:T(8,128)S(1)} fusion(bf16[64,16,3584]{2,1,0:T(8,128)(2,1)} %all-gather.5.cloned.1.call-done, bf16[256,3584]{1,0:T(8,128)(2,1)S(1)} %copy-done, f32[256,64]{0,1:T(8,128)S(1)} %get-tuple-element.6), kind=kOutput, calls=%fused_computation.14 | convolution fusion | flops 1879568384 | bytes 9256960 | tf_op jit(solution)/shard_map/dot_general | solution.py:13
  130.3 30.3 %all-reduce = (bf16[256,16]{0,1:T(8,128)(2,1)S(1)}, bf16[256,16]{0,1:T(8,128)(2,1)S(1)}) all-reduce(f32[256,16]{0,1:T(8,128)S(1)} %fusion.16, f32[256,16]{0,1:T(8,128)S(1)} %fusion.19), channel_id=1, replica_groups=mesh['dp'=32,'tensor'=8] {'tensor'}, use_global_device_ids=true, to_apply=%region_2.3 | all-reduce | flops 8192 | bytes 49152 | tf_op jit(solution)/shard_map/psum | solution.py:40
  160.6 2.0 convolution_convert_fusion.1
  162.7 0.0 reduce-scatter.5.cloned.1.call-update
  162.7 0.0 reduce-scatter.3.cloned.1.call-start
  162.8 5.1 %convolution_convert_fusion = bf16[64,16,3584]{2,1,0:T(8,128)(2,1)} fusion(bf16[256,3584]{1,0:T(8,128)(2,1)S(1)} %copy-done, bf16[256,16]{0,1:T(8,128)(2,1)S(1)} %get-tuple-element.3, bf16[256,64]{0,1:T(8,128)(2,1)S(1)} %get-tuple-element.5), kind=kOutput, calls=%fused_computation | convolution fusion | flops 1882980352 | bytes 9216000 | tf_op jit(solution)/shard_map/dot_general | solution.py:59
  167.9 0.6 copy-done.2
  168.5 0.1 select_reduce_fusion.1
  168.6 0.1 dynamic_slice.3
  168.7 6.5 %fusion.3 = bf16[256,3584]{1,0:T(8,128)(2,1)} fusion(bf16[64,16,3584]{2,1,0:T(8,128)(2,1)} %all-gather.5.cloned.1.call-done, bf16[256,16]{0,1:T(8,128)(2,1)S(1)} %get-tuple-element.3, bf16[256,64]{0,1:T(8,128)(2,1)S(1)} %get-tuple-element.5), kind=kOutput, calls=%fused_computation.5 | convolution fusion | flops 1881145344 | bytes 9216000 | tf_op jit(solution)/shard_map/dot_general | solution.py:48
  175.2 70.9 %reduce-scatter.5.cloned.1.call-done = bf16[2,16,1024]{2,1,0:T(8,128)(2,1)} async-done(((bf16[64,16,1024]{2,1,0:T(8,128)(2,1)}), bf16[2,16,1024]{2,1,0:T(8,128)(2,1)}) %reduce-scatter.5.cloned.1.call-update) | async-done | bytes 65552 | tf_op jit(solution)/shard_map/reduce_scatter | solution.py:75
  246.1 1.6 convert_multiply_fusion.1
  247.7 97.9 %reduce-scatter.3.cloned.1.call-done = bf16[2,16,3584]{2,1,0:T(8,128)(2,1)} async-done(((bf16[64,16,3584]{2,1,0:T(8,128)(2,1)}), bf16[2,16,3584]{2,1,0:T(8,128)(2,1)}) %reduce-scatter.3.cloned.1.call-update) | async-done | bytes 229392 | tf_op jit(solution)/shard_map/reduce_scatter | solution.py:67
  345.6 1.8 convert_multiply_fusion
  (11 shorter events, 0.1 us)
Async XLA Ops:
  7.2 112.2 %copy-start = (bf16[256,3584]{1,0:T(8,128)(2,1)S(1)}, bf16[256,3584]{1,0:T(8,128)(2,1)}, u32[]{:S(2)}) copy-start(bf16[256,3584]{1,0:T(8,128)(2,1)} %param.8) | copy-start | bytes 5505028
  7.2 54.6 %all-gather.3.cloned.1.call-start = ((), (), s32[]{:S(2)}) async-start(), calls=%async_computation.2 | async-start | bytes 2162688 | tf_op jit(solution)/shard_map/all_gather | solution.py:38
  7.9 111.5 %all-gather.5.cloned.1.call-start = ((), (), s32[]{:S(2)}) async-start(), calls=%async_computation.3 | async-start | bytes 7569408 | tf_op jit(solution)/shard_map/all_gather | solution.py:42
  8.7 237.5 %reduce-scatter.5.cloned.1.call-start = ((), (), s32[]{:S(2)}) async-start(), calls=%async_computation.5 | async-start | bytes 2162688 | tf_op jit(solution)/shard_map/reduce_scatter | solution.py:75
  66.0 94.6 %copy-start.1 = (bf16[256,1024]{1,0:T(8,128)(2,1)S(1)}, bf16[256,1024]{1,0:T(8,128)(2,1)}, u32[]{:S(2)}) copy-start(bf16[256,1024]{1,0:T(8,128)(2,1)} %param.7) | copy-start | bytes 1572868
  162.7 182.9 %reduce-scatter.3.cloned.1.call-start = ((), (), s32[]{:S(2)}) async-start(), calls=%async_computation.4 | async-start | bytes 7569408 | tf_op jit(solution)/shard_map/reduce_scatter | solution.py:67
  167.9 0.7 copy-start.2
  167.9 0.7 copy-start.3
Sparse Core Ops, SparseCore 0:
  10.5 51.1 all-gather.2
  64.3 55.0 all-gather.4
  162.8 83.2 reduce-scatter.4
  250.0 95.5 reduce-scatter.2
where the time goes:
time: 354 us
  waiting for transfers between devices  275 us (78%)
  blocking collectives  30.3 us (9%)
  matrix products  28.8 us (8%)
  between operations  13.8 us (4%)
  other arithmetic  4.95 us (1%)
    reduce_scatter x1, waiting for transfers between devices, on_device(): lax.psum_scatter(slot_term(broadcast_up, hidden, slots_per_worker * lax.a...  97.9 us
    reduce_scatter x1, waiting for transfers between devices, on_device(): lax.psum_scatter(slot_term(broadcast_down, output_gradient, slots_per_wor...  70.9 us
    all_gather x1, waiting for transfers between devices, on_device(): shard_portion = lax.all_gather(adapter_down, 'dp', axis=0, tiled=True)  53.4 us
    all_gather x1, waiting for transfers between devices, on_device(): lax.all_gather(adapter_up, 'dp', axis=0, tiled=True)  51.6 us
    psum x1, blocking collectives, on_device(): up_incoming = lax.psum(up_portion, 'tensor').astype(jnp.bfloat16)  30.3 us
    dot_general x2, matrix products, selected_rows(): lax.dot_general(value_entries, flattened_rows, (((1,), (1,)), ((), ())),...  15.2 us
    dot_general x2, matrix products, slot_term(): lax.dot_general(broadcast_portion, value_entries, (((0,), (0,)), ((), ())...  7.15 us
  transfers between devices with their start and end apart: 4, of which 4 were waited for; matrix products, arithmetic and copies ran while one was open for 5% of the time, Pallas kernels for 0%

commit v1 on v0

--- a/solution.py
+++ b/solution.py
@@ -35,7 +35,11 @@
     columns = lax.broadcasted_iota(jnp.int32, (1, adapter_list), 1)
     member_rows = (slot_of_row[:, None] == columns).astype(jnp.bfloat16)
     up_portion = selected_rows(
-        output_gradient, lax.all_gather(adapter_up, "dp", axis=0, tiled=True), member_rows
+        output_gradient,
+        jnp.concatenate(
+            lax.all_to_all(jnp.stack([adapter_up] * lax.axis_size("dp")), "dp", 0, 0), axis=0
+        ),
+        member_rows,
     )
     up_incoming = lax.psum(up_portion, "tensor").astype(jnp.bfloat16)
     broadcast_up = member_rows[:, :, None] * up_incoming[:, None, :]

time: 354 us -> 317 us (0.90)
  waiting for transfers between devices: 275 us -> 220 us
  local copies, waits for them, and re-layouts: 0.74 us -> 13.3 us
  starting transfers between devices: 0.16 us -> 8.11 us
    all_gather x1 -> x0, waiting for transfers between devices: 51.6 us -> none  [on_device(): lax.all_gather(adapter_up, 'dp', axis=0, tiled=True)]
    all_gather x1, waiting for transfers between devices: 53.4 us -> 20.8 us  [on_device(): shard_portion = lax.all_gather(adapter_down, 'dp', axis=0, tiled=True)]
    all_to_all x0 -> x1, waiting for transfers between devices: none -> 29.2 us  [on_device(): lax.all_to_all(jnp.stack([adapter_up] * lax.axis_size('dp')), 'dp', 0, 0)]
    all_to_all x0 -> x1, starting transfers between devices: none -> 7.81 us  [on_device(): lax.all_to_all(jnp.stack([adapter_up] * lax.axis_size('dp')), 'dp', 0, 0)]
    all_to_all x0 -> x1, local copies, waits for them, and re-layouts: none -> 4.84 us  [on_device(): lax.all_to_all(jnp.stack([adapter_up] * lax.axis_size('dp')), 'dp', 0, 0)]
    dot_general x0 -> x1, local copies, waits for them, and re-layouts: none -> 4.23 us  [selected_rows(): lax.dot_general(value_entries, flattened_rows, (((1,), (1,)), ((), ())),...]
  transfers between devices with their start and end apart: 4 -> 4, of which waited for: 4 -> 4; matrix products, arithmetic and copies ran while one was open for 5% -> 9% of each run, Pallas kernels for 0% -> 0%
where the time goes in v1:
time: 317 us; the launch traced here: 316 us
  waiting for transfers between devices  220 us (69%)
  blocking collectives  30.2 us (10%)
  matrix products  26.9 us (8%)
  between operations  13.8 us (4%)
  local copies, waits for them, and re-layouts  13.3 us (4%)
  starting transfers between devices  8.11 us (3%)
  other arithmetic  3.61 us (1%)
    reduce_scatter x1, waiting for transfers between devices, on_device(): lax.psum_scatter(slot_term(broadcast_up, hidden, slots_per_worker * lax.a...  98 us
    reduce_scatter x1, waiting for transfers between devices, on_device(): lax.psum_scatter(slot_term(broadcast_down, output_gradient, slots_per_wor...  71.4 us
    psum x1, blocking collectives, on_device(): up_incoming = lax.psum(up_portion, 'tensor').astype(jnp.bfloat16)  30.2 us
    all_to_all x1, waiting for transfers between devices, on_device(): lax.all_to_all(jnp.stack([adapter_up] * lax.axis_size('dp')), 'dp', 0, 0)  29.2 us
    all_gather x1, waiting for transfers between devices, on_device(): shard_portion = lax.all_gather(adapter_down, 'dp', axis=0, tiled=True)  20.8 us
    dot_general x2, matrix products, selected_rows(): lax.dot_general(value_entries, flattened_rows, (((1,), (1,)), ((), ())),...  13.3 us
    all_to_all x1, starting transfers between devices, on_device(): lax.all_to_all(jnp.stack([adapter_up] * lax.axis_size('dp')), 'dp', 0, 0)  7.81 us
    dot_general x2, matrix products, slot_term(): lax.dot_general(broadcast_portion, value_entries, (((0,), (0,)), ((), ())...  7.15 us
  transfers between devices with their start and end apart: 4, of which 4 were waited for; matrix products, arithmetic and copies ran while one was open for 9% of the time, Pallas kernels for 0%

profile of v1, /device:TPU:2, one launch (start us, length us, event | category | flops | bytes accessed | tf_op | source)
XLA Modules:
  0.0 316.1 jit_solution(6398795008330522139)
XLA Ops:
  7.2 0.0 all-gather.2.cloned.1.call-start
  7.2 0.7 all-gather.2.cloned.1.call-update
  7.9 0.9 copy.18
  8.8 3.2 %stack.2 = bf16[32,2,16,1024]{3,1,2,0:T(2,128)(2,1)} broadcast(bf16[2,16,1024]{2,0,1:T(2,128)(2,1)S(1)} %copy.18), dimensions={1,2,3} | broadcast | bytes 2162688 | tf_op jit(solution)/shard_map/stack | solution.py:40
  12.0 7.8 %all-to-all-start = ((bf16[32,2,16,1024]{3,1,2,0:T(2,128)(2,1)}), bf16[32,2,16,1024]{3,1,2,0:T(2,128)(2,1)}, u32[]{:S(2)}, u32[]{:S(2)}) async-start(bf16[32,2,16,1024]{3,1,2,0:T(2,128)(2,1)} %stack.2), calls=%async_computation | async-start | bytes 4194304 | tf_op jit(solution)/shard_map/all_to_all | solution.py:40
  19.8 0.0 reduce-scatter.5.cloned.1.call-start
  20.0 0.1 select_reduce_fusion
  20.1 29.2 %all-to-all-done = bf16[32,2,16,1024]{3,1,2,0:T(2,128)(2,1)} async-done(((bf16[32,2,16,1024]{3,1,2,0:T(2,128)(2,1)}), bf16[32,2,16,1024]{3,1,2,0:T(2,128)(2,1)}, u32[]{:S(2)}, u32[]{:S(2)}) %all-to-all-start) | async-done | bytes 2097184 | tf_op jit(solution)/shard_map/all_to_all | solution.py:40
  49.3 4.8 %copy.19 = bf16[32,2,16,1024]{3,1,0,2:T(2,128)(2,1)} copy(bf16[32,2,16,1024]{3,1,2,0:T(2,128)(2,1)} %all-to-all-done) | data formatting | bytes 4194304 | tf_op jit(solution)/shard_map/all_to_all | solution.py:40
  54.1 4.2 %dot_general.25 = bf16[64,16,1024]{2,0,1:T(8,128)(2,1)} reshape(bf16[32,2,16,1024]{3,1,0,2:T(2,128)(2,1)} %copy.19) | data formatting | bytes 4194304 | tf_op jit(solution)/shard_map/dot_general | solution.py:13
  58.4 2.3 fusion.11
  60.7 20.8 %all-gather.2.cloned.1.call-done = bf16[64,16,3584]{2,1,0:T(8,128)(2,1)} async-done(((bf16[2,16,3584]{2,1,0:T(8,128)(2,1)}), bf16[64,16,3584]{2,1,0:T(8,128)(2,1)}) %all-gather.2.cloned.1.call-update) | async-done | bytes 7340048 | tf_op jit(solution)/shard_map/all_gather | solution.py:46
  81.5 11.0 %fusion.12 = f32[256,16]{0,1:T(8,128)S(1)} fusion(bf16[64,16,3584]{2,1,0:T(8,128)(2,1)} %all-gather.2.cloned.1.call-done, bf16[256,3584]{1,0:T(8,128)(2,1)S(1)} %copy-done, f32[256,64]{0,1:T(8,128)S(1)} %get-tuple-element.6), kind=kOutput, calls=%fused_computation.12 | convolution fusion | flops 1879568384 | bytes 9256960 | tf_op jit(solution)/shard_map/dot_general | solution.py:13
  92.4 30.2 %all-reduce = (bf16[256,16]{0,1:T(8,128)(2,1)S(1)}, bf16[256,16]{0,1:T(8,128)(2,1)S(1)}) all-reduce(f32[256,16]{0,1:T(8,128)S(1)} %fusion.11, f32[256,16]{0,1:T(8,128)S(1)} %fusion.12), channel_id=1, replica_groups=mesh['dp'=32,'tensor'=8] {'tensor'}, use_global_device_ids=true, to_apply=%region_2.3 | all-reduce | flops 8192 | bytes 49152 | tf_op jit(solution)/shard_map/psum | solution.py:44
  122.7 2.0 convolution_convert_fusion.1
  124.8 0.2 reduce-scatter.3.cloned.1.call-start
  125.0 5.1 %convolution_convert_fusion = bf16[64,16,3584]{2,1,0:T(8,128)(2,1)} fusion(bf16[256,3584]{1,0:T(8,128)(2,1)S(1)} %copy-done, bf16[256,16]{0,1:T(8,128)(2,1)S(1)} %get-tuple-element.3, bf16[256,64]{0,1:T(8,128)(2,1)S(1)} %get-tuple-element.5), kind=kOutput, calls=%fused_computation | convolution fusion | flops 1882980352 | bytes 9216000 | tf_op jit(solution)/shard_map/dot_general | solution.py:63
  130.1 0.1 select_reduce_fusion.1
  130.2 0.1 dynamic_slice.3
  130.3 6.5 %fusion.3 = bf16[256,3584]{1,0:T(8,128)(2,1)} fusion(bf16[64,16,3584]{2,1,0:T(8,128)(2,1)} %all-gather.2.cloned.1.call-done, bf16[256,16]{0,1:T(8,128)(2,1)S(1)} %get-tuple-element.3, bf16[256,64]{0,1:T(8,128)(2,1)S(1)} %get-tuple-element.5), kind=kOutput, calls=%fused_computation.5 | convolution fusion | flops 1881145344 | bytes 9216000 | tf_op jit(solution)/shard_map/dot_general | solution.py:52
  136.8 71.4 %reduce-scatter.5.cloned.1.call-done = bf16[2,16,1024]{2,1,0:T(8,128)(2,1)} async-done(((bf16[64,16,1024]{2,1,0:T(8,128)(2,1)}), bf16[2,16,1024]{2,1,0:T(8,128)(2,1)}) %reduce-scatter.5.cloned.1.call-update) | async-done | bytes 65552 | tf_op jit(solution)/shard_map/reduce_scatter | solution.py:79
  208.2 1.6 convert_multiply_fusion.1
  209.8 98.0 %reduce-scatter.3.cloned.1.call-done = bf16[2,16,3584]{2,1,0:T(8,128)(2,1)} async-done(((bf16[64,16,3584]{2,1,0:T(8,128)(2,1)}), bf16[2,16,3584]{2,1,0:T(8,128)(2,1)}) %reduce-scatter.3.cloned.1.call-update) | async-done | bytes 229392 | tf_op jit(solution)/shard_map/reduce_scatter | solution.py:71
  307.8 1.8 convert_multiply_fusion
  (16 shorter events, 0.1 us)
Async XLA Ops:
  7.2 74.3 %copy-start = (bf16[256,3584]{1,0:T(8,128)(2,1)S(1)}, bf16[256,3584]{1,0:T(8,128)(2,1)}, u32[]{:S(2)}) copy-start(bf16[256,3584]{1,0:T(8,128)(2,1)} %param.8) | copy-start | bytes 5505028
  7.2 74.3 %all-gather.2.cloned.1.call-start = ((), (), s32[]{:S(2)}) async-start(), calls=%async_computation.3 | async-start | bytes 7569408 | tf_op jit(solution)/shard_map/all_gather | solution.py:46
  12.0 7.9 %copy-start.2 = (s32[64]{0:T(128)S(1)}, s32[64]{0:T(128)}, u32[]{:S(2)}) copy-start(s32[64]{0:T(128)} %param.12) | copy-start | bytes 772
  12.0 7.9 %copy-start.4 = (s32[64]{0:T(128)S(1)}, s32[64]{0:T(128)}, u32[]{:S(2)}) copy-start(s32[64]{0:T(128)} %param.11) | copy-start | bytes 772
  12.0 7.9 %copy-start.3 = (s32[64]{0:T(128)S(1)}, s32[64]{0:T(128)}, u32[]{:S(2)}) copy-start(s32[64]{0:T(128)} %param.13) | copy-start | bytes 772
  12.0 37.2 %all-to-all-start = ((bf16[32,2,16,1024]{3,1,2,0:T(2,128)(2,1)}), bf16[32,2,16,1024]{3,1,2,0:T(2,128)(2,1)}, u32[]{:S(2)}, u32[]{:S(2)}) async-start(bf16[32,2,16,1024]{3,1,2,0:T(2,128)(2,1)} %stack.2), calls=%async_computation | async-start | bytes 4194304 | tf_op jit(solution)/shard_map/all_to_all | solution.py:40
  19.8 188.4 %reduce-scatter.5.cloned.1.call-start = ((), (), s32[]{:S(2)}) async-start(), calls=%async_computation.5 | async-start | bytes 2162688 | tf_op jit(solution)/shard_map/reduce_scatter | solution.py:79
  54.1 4.2 %copy-start.1 = (bf16[256,1024]{1,0:T(8,128)(2,1)S(1)}, bf16[256,1024]{1,0:T(8,128)(2,1)}, u32[]{:S(2)}) copy-start(bf16[256,1024]{1,0:T(8,128)(2,1)} %param.7) | copy-start | bytes 1572868
  124.8 183.1 %reduce-scatter.3.cloned.1.call-start = ((), (), s32[]{:S(2)}) async-start(), calls=%async_computation.4 | async-start | bytes 7569408 | tf_op jit(solution)/shard_map/reduce_scatter | solution.py:71
Sparse Core Ops, SparseCore 0:
  10.5 70.9 all-gather.1
  124.9 83.2 reduce-scatter.4
  212.3 95.4 reduce-scatter.2
